TPU v7x, 128 devices: a whole 4x4x4 slice. The times are simulated.
128 devices in a mesh: seq: 32 (over z, x, core), exp: 4 (over y).
Axes of the slice: x: 4, y: 4, z: 4, core: 2. Of those that a mesh axis runs over, the one named last changes fastest.
Arguments:
- queries: bfloat16 [4096, 5120], P('seq', 'exp'), may hold values from -48 to 48
- keys_values: bfloat16 [2, 4096, 1024], P(None, 'seq', 'exp'), may hold values from -8 to 8
- residual: bfloat16 [4096, 5120], P(('seq', 'exp')), may hold values from -6 to 6
- norm_gain: float32 [5120], replicated, may hold values from 0.1 to 1.9
- route_logit: float32 [4096], P(('seq', 'exp')), may hold values from -2 to -1
- expert_ids: int32 [4096, 1], P(('seq', 'exp')), may hold values from 0 to 3; in each aligned block of 32 rows (0 to 31, 32 to 63, ...) at most 12 rows name the same one
- out_weight: bfloat16 [5120, 5120], P('exp'), may hold values from -0.078125 to 0.078125
- gate_weight: bfloat16 [4, 5120, 8192], P('exp', None, 'seq'), may hold values from -0.25 to 0.25
- up_weight: bfloat16 [4, 5120, 8192], P('exp', None, 'seq'), may hold values from -0.25 to 0.25
- down_weight: bfloat16 [4, 8192, 5120], P('exp', 'seq'), may hold values from -0.125 to 0.125
Outputs:
- layer_output: bfloat16 [4096, 5120], P(('seq', 'exp'))
Inputs may be any that keep to these rules, and one draw needn't show every extreme that they name: `expert_ids`: in each aligned block of 32 tokens (the tokens of one device) no expert is named more than 12 times, a bound that some block reaches.
All inputs are finite; a program needn't handle non-finite values.
Results may differ from a plain program's by a relative error of at most 0.015.
Values may be sent and summed in bfloat16 or wider, within the bound.
No kernel may reach another device: no remote copies, remote signals or barrier semaphores. Data moves between devices by JAX's collectives and lax.ppermute only.
A program may use at most 128 MiB of HBM per device.

v0:
```python
import jax
import jax.numpy as jnp
from jax import lax
from jax.sharding import PartitionSpec as P

D = 5120
HD = 128


def in_blocks(shard, dim, devices):
    dims = shard.shape
    parts = shard.reshape(*dims[:dim], devices, dims[dim] // devices, *dims[dim + 1 :])
    return jnp.moveaxis(parts, dim, 0)


def sent_and_summed(shard, axis, dim):
    devices = lax.axis_size(axis)
    parts = lax.all_to_all(in_blocks(shard, dim, devices), axis, 0, 0, tiled=True)
    return jnp.sum(parts.astype(jnp.float32), axis=0)


def body(
    queries,
    keys_values,
    residual,
    norm_gain,
    route_logit,
    expert_ids,
    out_weight,
    gate_weight,
    up_weight,
    down_weight,
):
    seq_rows = queries.shape[0]
    heads_here = queries.shape[1] // HD
    kv_here = keys_values.shape[2] // HD
    group = heads_here // kv_here
    seq_index = lax.axis_index("seq")
    span_devs = lax.axis_size("seq")
    my_position = seq_index * seq_rows + jnp.arange(seq_rows, dtype=jnp.int32)
    my_span = seq_index // span_devs
    scale = 1.0 / HD**0.5
    query_heads = queries.reshape(seq_rows, kv_here, group, HD)
    piece = lax.all_gather(keys_values, "seq", axis=1, tiled=True)
    peak = jnp.full((kv_here, group, seq_rows), -1e30, jnp.float32)
    count = piece.shape[1]
    key_position = jnp.arange(count, dtype=jnp.int32)
    same_span = key_position // (span_devs * seq_rows) == my_span
    allowed = same_span[None, :] & (key_position[None, :] <= my_position[:, None])
    key_rows = piece[0].reshape(count, kv_here, HD)
    value_rows = piece[1].reshape(count, kv_here, HD)
    score = (
        jnp.einsum("skgd,nkd->kgsn", query_heads, key_rows, preferred_element_type=jnp.float32)
        * scale
    )
    score = jnp.where(allowed, score, -1e30)
    fresh = jnp.maximum(peak, jnp.max(score, axis=-1))
    expo = jnp.where(allowed, jnp.exp(score - fresh[..., None]), 0.0)
    total = jnp.sum(expo, axis=-1)
    accum = jnp.einsum(
        "kgsn,nkd->kgsd", expo.astype(jnp.bfloat16), value_rows, preferred_element_type=jnp.float32
    )
    state = (fresh, total, accum)
    peak, total, accum = state
    attended = (
        jnp.transpose(accum / total[..., None], (2, 0, 1, 3))
        .reshape(seq_rows, heads_here * HD)
        .astype(jnp.bfloat16)
    )
    rows = attended
    projected = sent_and_summed(
        jnp.dot(rows, out_weight, preferred_element_type=jnp.float32).astype(jnp.bfloat16), "exp", 0
    )
    stream = residual.astype(jnp.float32) + projected
    mixed = stream.astype(jnp.bfloat16)
    stream = mixed.astype(jnp.float32)
    mean_square = jnp.mean(stream * stream, axis=-1, keepdims=True)
    routed_in = (
        stream * lax.rsqrt(mean_square + 1e-05) * norm_gain * jax.nn.sigmoid(route_logit)[:, None]
    ).astype(jnp.bfloat16)
    token_rows = residual.shape[0]
    capacity = 3 * token_rows // 8
    experts = lax.axis_size("exp")
    ids = expert_ids[:, 0]
    onehot = (ids[:, None] == jnp.arange(experts, dtype=jnp.int32)[None, :]).astype(jnp.int32)
    rank = jnp.sum((jnp.cumsum(onehot, axis=0) - onehot) * onehot, axis=1)
    slot = ids * capacity + rank
    placing = (jnp.arange(experts * capacity, dtype=jnp.int32)[:, None] == slot[None, :]).astype(
        jnp.bfloat16
    )
    outgoing = (
        jnp.dot(placing, routed_in, preferred_element_type=jnp.float32)
        .astype(jnp.bfloat16)
        .reshape(experts, capacity, D)
    )
    arrived = lax.all_to_all(outgoing, "exp", split_axis=0, concat_axis=0, tiled=True).reshape(
        experts * capacity, D
    )
    piece = lax.all_gather(arrived, "seq", axis=0, tiled=True)
    gate = jnp.dot(piece, gate_weight[0], preferred_element_type=jnp.float32)
    up = jnp.dot(piece, up_weight[0], preferred_element_type=jnp.float32)
    hidden = (jax.nn.silu(gate) * up).astype(jnp.bfloat16)
    rows = hidden
    summed = lax.psum_scatter(
        jnp.dot(rows, down_weight[0], preferred_element_type=jnp.float32).astype(jnp.bfloat16),
        "seq",
        scatter_dimension=0,
        tiled=True,
    )
    returned = lax.all_to_all(
        summed.reshape(experts, capacity, D), "exp", split_axis=0, concat_axis=0, tiled=True
    )
    back_rows = returned.reshape(experts * capacity, D)
    picking = (slot[:, None] == jnp.arange(experts * capacity, dtype=jnp.int32)[None, :]).astype(
        jnp.bfloat16
    )
    routed = jnp.dot(picking, back_rows, preferred_element_type=jnp.float32)
    return (stream + routed).astype(jnp.bfloat16)


def solution(mesh):
    in_specs = (
        P("seq", "exp"),
        P(None, "seq", "exp"),
        P(("seq", "exp"), None),
        P(),
        P(("seq", "exp")),
        P(("seq", "exp"), None),
        P("exp", None),
        P("exp", None, "seq"),
        P("exp", None, "seq"),
        P("exp", "seq", None),
    )
    out_specs = P(("seq", "exp"), None)
    return jax.shard_map(body, mesh=mesh, in_specs=in_specs, out_specs=out_specs, check_vma=False)
```

profile of v0, /device:TPU:0, one launch (start us, length us, event | category | flops | bytes accessed | tf_op | source)
XLA Modules:
  0.0 383.5 jit_solution(18373603022265235883)
XLA Ops:
  6.5 1.8 copy.14
  8.4 1.9 copy.15
  10.3 2.1 fusion.14
  12.4 48.3 %all-gather.3.cloned.1.call-done = bf16[2,4096,256]{1,2,0:T(8,128)(2,1)} async-done(((bf16[2,128,256]{1,2,0:T(8,128)(2,1)}), bf16[2,4096,256]{1,2,0:T(8,128)(2,1)}) %all-gather.3.cloned.1.call-update) | async-done | bytes 4194320 | tf_op jit(solution)/shard_map/all_gather | solution.py:44
  60.8 4.7 %fusion.47 = (bf16[1,4096,256]{1,2,0:T(8,128)(2,1)}, bf16[1,4096,256]{1,2,0:T(8,128)(2,1)}) fusion(bf16[2,4096,256]{1,2,0:T(8,128)(2,1)} %all-gather.3.cloned.1.call-done), kind=kLoop, calls=%fused_computation.61 | loop fusion | bytes 8388608 | tf_op jit(solution)/shard_map/slice | solution.py:50
  65.5 5.0 %fusion = (f32[2,5,128]{2,1,0:T(8,128)S(1)}, f32[2,4096,128,5]{2,1,3,0:T(8,128)S(1)}) fusion(pred[128,4096]{0,1:T(8,128)(4,1)S(1)} %fusion.14, bf16[4096,2,128,1]{0,2,3,1:T(8,128)(2,1)} %bitcast.66, bf16[128,2,5,128]{0,3,2,1:T(8,128)(2,1)} %bitcast.69), kind=kOutput, calls=%fused_computation.3 | convolution fusion | flops 1357904640 | bytes 23925760 | tf_op jit(solution)/shard_map/skgd,nkd->kgsn/dot_general | solution.py:53
  70.5 5.1 %fusion.1 = f32[2,5,128]{2,1,0:T(8,128)S(1)} fusion(f32[2,4096,128,5]{2,1,3,0:T(8,128)S(1)} %get-tuple-element.10, f32[2,5,128]{2,1,0:T(8,128)S(1)} %broadcast_maximum_fusion, pred[128,4096]{0,1:T(8,128)(4,1)S(1)} %fusion.14), kind=kLoop, calls=%fused_computation.4 | loop fusion | flops 26213120 | bytes 21506048 | tf_op jit(solution)/shard_map/reduce_sum | solution.py:59
  75.6 1.9 copy-done.1
  77.5 13.1 %fusion.21 = bf16[128,2,5,128]{0,3,2,1:T(8,128)(2,1)S(1)} fusion(bf16[4096,2,128,1]{0,2,3,1:T(8,128)(2,1)} %bitcast.68, f32[2,4096,128,5]{2,1,3,0:T(8,128)} %copy-done.1, f32[2,5,128]{2,1,0:T(8,128)S(1)} %broadcast_maximum_fusion, pred[128,4096]{0,1:T(8,128)(4,1)S(1)} %fusion.14, f32[128,2,5]{0,2,1:T(8,128)S(1)} %bitcast.71), kind=kOutput, calls=%fused_computation.23 | convolution fusion | flops 1368719360 | bytes 23930880 | tf_op jit(solution)/shard_map/kgsn,nkd->kgsd/dot_general | solution.py:60
  90.6 7.8 %convolution_convert_fusion.1 = bf16[128,5120]{1,0:T(8,128)(2,1)} fusion(bf16[128,1280]{0,1:T(8,128)(2,1)S(1)} %bitcast.70, bf16[1280,5120]{1,0:T(8,128)(2,1)} %param.16), kind=kOutput, calls=%fused_computation.8 | convolution fusion | flops 1678376960 | bytes 14745600 | tf_op jit(solution)/shard_map/dot_general | solution.py:72
  98.4 4.4 %all-to-all-start = ((bf16[4,32,5120]{2,1,0:T(8,128)(2,1)}), bf16[4,32,5120]{2,1,0:T(8,128)(2,1)}, u32[]{:S(2)}, u32[]{:S(2)}) async-start(bf16[4,32,5120]{2,1,0:T(8,128)(2,1)} %bitcast.67), calls=%async_computation | async-start | bytes 2621440 | tf_op jit(solution)/shard_map/all_to_all | solution.py:18
  103.3 18.1 %all-to-all-done = bf16[4,32,5120]{2,1,0:T(8,128)(2,1)} async-done(((bf16[4,32,5120]{2,1,0:T(8,128)(2,1)}), bf16[4,32,5120]{2,1,0:T(8,128)(2,1)}, u32[]{:S(2)}, u32[]{:S(2)}) %all-to-all-start) | async-done | bytes 1310752 | tf_op jit(solution)/shard_map/all_to_all | solution.py:18
  121.4 1.6 convert_reduce_fusion
  125.1 1.1 reshape.63
  126.3 13.8 %all_to_all.15 = bf16[4,12,5120]{2,1,0:T(8,128)(2,1)} all-to-all(bf16[4,12,5120]{2,1,0:T(8,128)(2,1)S(1)} %reshape.63), channel_id=1, replica_groups=mesh['seq'=32,'exp'=4] {'exp'}, dimensions={0} | all-to-all | bytes 983040 | tf_op jit(solution)/shard_map/all_to_all | solution.py:96
  140.0 2.0 reshape.64
  142.1 68.0 %all-gather.5.cloned.1.call-done = bf16[1536,5120]{1,0:T(8,128)(2,1)} async-done(((bf16[48,5120]{1,0:T(8,128)(2,1)}), bf16[1536,5120]{1,0:T(8,128)(2,1)}) %all-gather.5.cloned.1.call-update) | async-done | bytes 15728656 | tf_op jit(solution)/shard_map/all_gather | solution.py:99
  210.1 11.7 %fusion.9 = f32[1536,256]{1,0:T(8,128)} fusion(bf16[1536,5120]{1,0:T(8,128)(2,1)} %all-gather.5.cloned.1.call-done, bf16[1,5120,256]{2,1,0:T(8,128)(2,1)} %param.17), kind=kOutput, calls=%fused_computation.15 | convolution fusion | flops 4026531840 | bytes 19922944 | tf_op jit(solution)/shard_map/dot_general | solution.py:100
  221.8 23.8 %convolution_convert_fusion = bf16[1536,5120]{1,0:T(8,128)(2,1)} fusion(bf16[1,256,5120]{2,1,0:T(8,128)(2,1)S(1)} %copy-done, bf16[1536,5120]{1,0:T(8,128)(2,1)} %all-gather.5.cloned.1.call-done, bf16[1,5120,256]{2,1,0:T(8,128)(2,1)} %param.18, f32[1536,256]{1,0:T(8,128)} %fusion.9), kind=kOutput, calls=%fused_computation.2 | convolution fusion | flops 8063287296 | bytes 38273024 | tf_op jit(solution)/shard_map/dot_general | solution.py:105
  245.6 112.5 %reduce-scatter.2.cloned.1.call-done = bf16[48,5120]{1,0:T(8,128)(2,1)} async-done(((bf16[1536,5120]{1,0:T(8,128)(2,1)}), bf16[48,5120]{1,0:T(8,128)(2,1)}) %reduce-scatter.2.cloned.1.call-update) | async-done | bytes 491536 | tf_op jit(solution)/shard_map/reduce_scatter | solution.py:104
  358.1 2.0 reshape.65
  360.1 4.3 %all-to-all-start.2 = ((bf16[4,12,5120]{2,1,0:T(8,128)(2,1)}), bf16[4,12,5120]{2,1,0:T(8,128)(2,1)S(1)}, u32[]{:S(2)}, u32[]{:S(2)}) async-start(bf16[4,12,5120]{2,1,0:T(8,128)(2,1)} %reshape.65), calls=%async_computation.3 | async-start | bytes 1310720 | tf_op jit(solution)/shard_map/all_to_all | solution.py:110
  364.4 9.6 %all-to-all-done.2 = bf16[4,12,5120]{2,1,0:T(8,128)(2,1)S(1)} async-done(((bf16[4,12,5120]{2,1,0:T(8,128)(2,1)}), bf16[4,12,5120]{2,1,0:T(8,128)(2,1)S(1)}, u32[]{:S(2)}, u32[]{:S(2)}) %all-to-all-start.2) | async-done | bytes 491552 | tf_op jit(solution)/shard_map/all_to_all | solution.py:110
  374.9 2.1 fusion.6
  (31 shorter events, 3.6 us)
Async XLA Ops:
  6.5 215.3 %copy-start = (bf16[1,256,5120]{2,1,0:T(8,128)(2,1)S(1)}, bf16[1,256,5120]{2,1,0:T(8,128)(2,1)}, u32[]{:S(2)}) copy-start(bf16[1,256,5120]{2,1,0:T(8,128)(2,1)} %param.19) | copy-start | bytes 7864324
  6.5 54.2 %all-gather.3.cloned.1.call-start = ((), (), s32[]{:S(2)}) async-start(), calls=%async_computation.4 | async-start | bytes 4325376 | tf_op jit(solution)/shard_map/all_gather | solution.py:44
  70.5 7.0 %copy-start.1 = (f32[2,4096,128,5]{2,1,3,0:T(8,128)}, f32[2,4096,128,5]{2,1,3,0:T(8,128)S(1)}, u32[]{:S(2)}) copy-start(f32[2,4096,128,5]{2,1,3,0:T(8,128)S(1)} %get-tuple-element.10) | copy-start | bytes 62914564
  90.5 12.5 %copy-start.4 = (s32[32,1]{0,1:T(1,128)S(1)}, s32[32,1]{0,1:T(1,128)}, u32[]{:S(2)}) copy-start(s32[32,1]{0,1:T(1,128)} %param.15) | copy-start | bytes 388
  90.6 32.5 %copy-start.3 = (bf16[32,5120]{1,0:T(8,128)(2,1)S(1)}, bf16[32,5120]{1,0:T(8,128)(2,1)}, u32[]{:S(2)}) copy-start(bf16[32,5120]{1,0:T(8,128)(2,1)} %param.12) | copy-start | bytes 983044
  98.3 24.9 %copy-start.5 = (f32[32]{0:T(128)S(1)}, f32[32]{0:T(128)}, u32[]{:S(2)}) copy-start(f32[32]{0:T(128)} %param.14) | copy-start | bytes 388
  98.3 25.6 %copy-start.6 = (f32[5120]{0:T(1024)S(1)}, f32[5120]{0:T(1024)}, u32[]{:S(2)}) copy-start(f32[5120]{0:T(1024)} %param.13) | copy-start | bytes 61444
  98.4 23.1 %all-to-all-start = ((bf16[4,32,5120]{2,1,0:T(8,128)(2,1)}), bf16[4,32,5120]{2,1,0:T(8,128)(2,1)}, u32[]{:S(2)}, u32[]{:S(2)}) async-start(bf16[4,32,5120]{2,1,0:T(8,128)(2,1)} %bitcast.67), calls=%async_computation | async-start | bytes 2621440 | tf_op jit(solution)/shard_map/all_to_all | solution.py:18
  102.8 107.3 %all-gather.5.cloned.1.call-start = ((), (), s32[]{:S(2)}) async-start(), calls=%async_computation.5 | async-start | bytes 16220160 | tf_op jit(solution)/shard_map/all_gather | solution.py:99
  123.3 0.7 copy-start.2
  142.0 216.1 %reduce-scatter.2.cloned.1.call-start = ((), (), s32[]{:S(2)}) async-start(), calls=%async_computation.6 | async-start | bytes 16220160 | tf_op jit(solution)/shard_map/reduce_scatter | solution.py:104
  360.1 13.9 %all-to-all-start.2 = ((bf16[4,12,5120]{2,1,0:T(8,128)(2,1)}), bf16[4,12,5120]{2,1,0:T(8,128)(2,1)S(1)}, u32[]{:S(2)}, u32[]{:S(2)}) async-start(bf16[4,12,5120]{2,1,0:T(8,128)(2,1)} %reshape.65), calls=%async_computation.3 | async-start | bytes 1310720 | tf_op jit(solution)/shard_map/all_to_all | solution.py:110
Sparse Core Ops, SparseCore 0:
  9.5 51.1 all-gather.2
  142.2 67.8 all-gather.4
  245.8 112.3 reduce-scatter.1
where the time goes:
time: 384 us
  waiting for transfers between devices  257 us (67%)
  matrix products  64.6 us (17%)
  local copies, waits for them, and re-layouts  17 us (4%)
  blocking collectives  13.8 us (4%)
  between operations  13.2 us (3%)
  other arithmetic  9.37 us (2%)
  starting transfers between devices  8.97 us (2%)
    reduce_scatter x1, waiting for transfers between devices, body(): lax.psum_scatter(jnp.dot(rows, down_weight[0], preferred_element_type=jnp...  112 us
    all_gather x1, waiting for transfers between devices, body(): piece = lax.all_gather(arrived, 'seq', axis=0, tiled=True)  68 us
    all_gather x1, waiting for transfers between devices, body(): piece = lax.all_gather(keys_values, 'seq', axis=1, tiled=True)  48.3 us
    dot_general x1, matrix products, body(): jnp.dot(rows, down_weight[0], preferred_element_type=jnp.float32)  23.8 us
    all_to_all x1, waiting for transfers between devices, sent_and_summed(): lax.all_to_all(in_blocks(shard, dim, devices), axis, 0, 0, tiled=True)  18.1 us
    all_to_all x1, blocking collectives, body(): lax.all_to_all(outgoing, 'exp', split_axis=0, concat_axis=0, tiled=True)  13.8 us
    dot_general x1, matrix products, body(): jnp.einsum('kgsn,nkd->kgsd', expo.astype(jnp.bfloat16), value_rows, prefe...  13.1 us
    dot_general x1, matrix products, body(): gate = jnp.dot(piece, gate_weight[0], preferred_element_type=jnp.float32)  11.7 us
  transfers between devices with their start and end apart: 5, of which 5 were waited for; matrix products, arithmetic and copies ran while one was open for 1% of the time, Pallas kernels for 0%

commit v1 on v0

--- a/solution.py
+++ b/solution.py
@@ -41,7 +41,10 @@
     my_span = seq_index // span_devs
     scale = 1.0 / HD**0.5
     query_heads = queries.reshape(seq_rows, kv_here, group, HD)
-    piece = lax.all_gather(keys_values, "seq", axis=1, tiled=True)
+    size = lax.axis_size("seq")
+    tiles = jnp.stack([keys_values for _ in range(size)])
+    tiles = lax.all_to_all(tiles, "seq", split_axis=0, concat_axis=0)
+    piece = jnp.concatenate(tiles, axis=1)
     peak = jnp.full((kv_here, group, seq_rows), -1e30, jnp.float32)
     count = piece.shape[1]
     key_position = jnp.arange(count, dtype=jnp.int32)

time: 384 us -> 409 us (1.065)
  local copies, waits for them, and re-layouts: 17 us -> 32.7 us
  starting transfers between devices: 8.97 us -> 17.7 us
    all_to_all x0 -> x1, waiting for transfers between devices: none -> 50.9 us  [body(): tiles = lax.all_to_all(tiles, 'seq', split_axis=0, concat_axis=0)]
    all_gather x1 -> x0, waiting for transfers between devices: 48.3 us -> none  [body(): piece = lax.all_gather(keys_values, 'seq', axis=1, tiled=True)]
    another operation x0 -> x3, local copies, waits for them, and re-layouts: none -> 11.3 us  [the longest x1 4.15 us: body(): key_rows = piece[0].reshape(count, kv_here, HD)]
    all_to_all x0 -> x1, starting transfers between devices: none -> 8.53 us  [body(): tiles = lax.all_to_all(tiles, 'seq', split_axis=0, concat_axis=0)]
    slice x0 -> x2, local copies, waits for them, and re-layouts: none -> 6.72 us  [body(): value_rows = piece[1].reshape(count, kv_here, HD)]
where the time goes in v1:
time: 409 us; the launch traced here: 408 us
  waiting for transfers between devices  258 us (63%)
  matrix products  64.6 us (16%)
  local copies, waits for them, and re-layouts  32.7 us (8%)
  starting transfers between devices  17.7 us (4%)
  between operations  13.5 us (3%)
  blocking collectives  11.9 us (3%)
  other arithmetic  9.55 us (2%)
    reduce_scatter x1, waiting for transfers between devices, body(): lax.psum_scatter(jnp.dot(rows, down_weight[0], preferred_element_type=jnp...  113 us
    all_gather x1, waiting for transfers between devices, body(): piece = lax.all_gather(arrived, 'seq', axis=0, tiled=True)  70.4 us
    all_to_all x1, waiting for transfers between devices, body(): tiles = lax.all_to_all(tiles, 'seq', split_axis=0, concat_axis=0)  50.9 us
    dot_general x1, matrix products, body(): jnp.dot(rows, down_weight[0], preferred_element_type=jnp.float32)  23.8 us
    all_to_all x1, waiting for transfers between devices, sent_and_summed(): lax.all_to_all(in_blocks(shard, dim, devices), axis, 0, 0, tiled=True)  14.8 us
    dot_general x1, matrix products, body(): jnp.einsum('kgsn,nkd->kgsd', expo.astype(jnp.bfloat16), value_rows, prefe...  13.1 us
    all_to_all x1, blocking collectives, body(): lax.all_to_all(outgoing, 'exp', split_axis=0, concat_axis=0, tiled=True)  11.9 us
    dot_general x1, matrix products, body(): gate = jnp.dot(piece, gate_weight[0], preferred_element_type=jnp.float32)  11.7 us
  transfers between devices with their start and end apart: 5, of which 5 were waited for; matrix products, arithmetic and copies ran while one was open for 1% of the time, Pallas kernels for 0%

profile of v1, /device:TPU:0, one launch (start us, length us, event | category | flops | bytes accessed | tf_op | source)
XLA Modules:
  0.0 408.2 jit_solution(10059108673750025196)
XLA Ops:
  7.7 3.0 stack.2
  10.7 8.5 %all-to-all-start = ((bf16[32,2,128,256]{2,3,1,0:T(8,128)(2,1)}), bf16[32,2,128,256]{2,3,1,0:T(8,128)(2,1)}, u32[]{:S(2)}, u32[]{:S(2)}) async-start(bf16[32,2,128,256]{2,3,1,0:T(8,128)(2,1)} %stack.2), calls=%async_computation | async-start | bytes 8388608 | tf_op jit(solution)/shard_map/all_to_all | solution.py:46
  20.2 2.1 fusion.17
  22.3 50.9 %all-to-all-done = bf16[32,2,128,256]{2,3,1,0:T(8,128)(2,1)} async-done(((bf16[32,2,128,256]{2,3,1,0:T(8,128)(2,1)}), bf16[32,2,128,256]{2,3,1,0:T(8,128)(2,1)}, u32[]{:S(2)}, u32[]{:S(2)}) %all-to-all-start) | async-done | bytes 4194336 | tf_op jit(solution)/shard_map/all_to_all | solution.py:46
  73.2 4.0 fusion.56
  77.2 2.7 copy.24
  79.9 4.1 %reshape.79 = bf16[4096,2,128,1]{0,2,1,3:T(8,128)(2,1)} reshape(bf16[1,32,128,256]{2,1,3,0:T(8,128)(2,1)} %copy.24) | data formatting | bytes 4194304 | tf_op jit(solution)/shard_map/reshape;squeeze | solution.py:54
  84.1 4.3 %copy.20 = bf16[1,32,128,256]{2,1,3,0:T(8,128)(2,1)} copy(bf16[1,32,128,256]{2,3,0,1:T(8,128)(2,1)} %get-tuple-element.8) | data formatting | bytes 4194304 | tf_op jit(solution)/shard_map/slice | solution.py:53
  88.3 4.1 %reshape_squeeze.6 = bf16[4096,2,128]{0,2,1:T(8,128)(2,1)} reshape(bf16[1,32,128,256]{2,1,3,0:T(8,128)(2,1)} %copy.20) | data formatting | bytes 4194304 | tf_op jit(solution)/shard_map/reshape;squeeze | solution.py:53
  92.5 5.0 %fusion = (f32[2,5,128]{2,1,0:T(8,128)S(1)}, f32[2,4096,128,5]{2,1,3,0:T(8,128)S(1)}) fusion(pred[128,4096]{0,1:T(8,128)(4,1)S(1)} %fusion.17, bf16[128,2,5,128]{0,3,2,1:T(8,128)(2,1)} %bitcast.80, bf16[4096,2,128]{0,2,1:T(8,128)(2,1)} %reshape_squeeze.6), kind=kOutput, calls=%fused_computation.3 | convolution fusion | flops 1357904640 | bytes 23925760 | tf_op jit(solution)/shard_map/skgd,nkd->kgsn/dot_general | solution.py:56
  97.5 5.3 %fusion.1 = f32[2,5,128]{2,1,0:T(8,128)S(1)} fusion(f32[2,4096,128,5]{2,1,3,0:T(8,128)S(1)} %get-tuple-element.10, f32[2,5,128]{2,1,0:T(8,128)S(1)} %broadcast_maximum_fusion, pred[128,4096]{0,1:T(8,128)(4,1)S(1)} %fusion.17), kind=kLoop, calls=%fused_computation.4 | loop fusion | flops 26213120 | bytes 21506048 | tf_op jit(solution)/shard_map/reduce_sum | solution.py:62
  104.5 13.1 %fusion.28 = bf16[128,2,5,128]{0,3,2,1:T(8,128)(2,1)S(1)} fusion(f32[2,4096,128,5]{2,1,3,0:T(8,128)} %copy-done.1, f32[2,5,128]{2,1,0:T(8,128)S(1)} %broadcast_maximum_fusion, pred[128,4096]{0,1:T(8,128)(4,1)S(1)} %fusion.17, bf16[4096,2,128,1]{0,2,1,3:T(8,128)(2,1)} %reshape.79, f32[128,2,5]{0,2,1:T(8,128)S(1)} %bitcast.82), kind=kOutput, calls=%fused_computation.26 | convolution fusion | flops 1368719360 | bytes 23930880 | tf_op jit(solution)/shard_map/kgsn,nkd->kgsd/dot_general | solution.py:63
  117.6 7.7 %convolution_convert_fusion.1 = bf16[128,5120]{1,0:T(8,128)(2,1)} fusion(bf16[128,1280]{0,1:T(8,128)(2,1)S(1)} %bitcast.81, bf16[1280,5120]{1,0:T(8,128)(2,1)} %param.16), kind=kOutput, calls=%fused_computation.8 | convolution fusion | flops 1678376960 | bytes 14745600 | tf_op jit(solution)/shard_map/dot_general | solution.py:75
  125.3 4.6 %all-to-all-start.1 = ((bf16[4,32,5120]{2,1,0:T(8,128)(2,1)}), bf16[4,32,5120]{2,1,0:T(8,128)(2,1)}, u32[]{:S(2)}, u32[]{:S(2)}) async-start(bf16[4,32,5120]{2,1,0:T(8,128)(2,1)} %bitcast.79), calls=%async_computation.1 | async-start | bytes 2621440 | tf_op jit(solution)/shard_map/all_to_all | solution.py:18
  130.2 14.8 %all-to-all-done.1 = bf16[4,32,5120]{2,1,0:T(8,128)(2,1)} async-done(((bf16[4,32,5120]{2,1,0:T(8,128)(2,1)}), bf16[4,32,5120]{2,1,0:T(8,128)(2,1)}, u32[]{:S(2)}, u32[]{:S(2)}) %all-to-all-start.1) | async-done | bytes 1310752 | tf_op jit(solution)/shard_map/all_to_all | solution.py:18
  149.9 11.9 %all_to_all.20 = bf16[4,12,5120]{2,1,0:T(8,128)(2,1)} all-to-all(bf16[4,12,5120]{2,1,0:T(8,128)(2,1)S(1)} %reshape.74), channel_id=1, replica_groups=mesh['seq'=32,'exp'=4] {'exp'}, dimensions={0} | all-to-all | bytes 983040 | tf_op jit(solution)/shard_map/all_to_all | solution.py:99
  161.8 2.0 reshape.75
  164.0 70.4 %all-gather.2.cloned.1.call-done = bf16[1536,5120]{1,0:T(8,128)(2,1)} async-done(((bf16[48,5120]{1,0:T(8,128)(2,1)}), bf16[1536,5120]{1,0:T(8,128)(2,1)}) %all-gather.2.cloned.1.call-update) | async-done | bytes 15728656 | tf_op jit(solution)/shard_map/all_gather | solution.py:102
  234.4 11.7 %fusion.9 = f32[1536,256]{1,0:T(8,128)} fusion(bf16[1536,5120]{1,0:T(8,128)(2,1)} %all-gather.2.cloned.1.call-done, bf16[1,5120,256]{2,1,0:T(8,128)(2,1)} %param.17), kind=kOutput, calls=%fused_computation.15 | convolution fusion | flops 4026531840 | bytes 19922944 | tf_op jit(solution)/shard_map/dot_general | solution.py:103
  246.1 23.8 %convolution_convert_fusion = bf16[1536,5120]{1,0:T(8,128)(2,1)} fusion(bf16[1,256,5120]{2,1,0:T(8,128)(2,1)S(1)} %copy-done, bf16[1536,5120]{1,0:T(8,128)(2,1)} %all-gather.2.cloned.1.call-done, bf16[1,5120,256]{2,1,0:T(8,128)(2,1)} %param.18, f32[1536,256]{1,0:T(8,128)} %fusion.9), kind=kOutput, calls=%fused_computation.2 | convolution fusion | flops 8063287296 | bytes 38273024 | tf_op jit(solution)/shard_map/dot_general | solution.py:108
  269.9 112.5 %reduce-scatter.2.cloned.1.call-done = bf16[48,5120]{1,0:T(8,128)(2,1)} async-done(((bf16[1536,5120]{1,0:T(8,128)(2,1)}), bf16[48,5120]{1,0:T(8,128)(2,1)}) %reduce-scatter.2.cloned.1.call-update) | async-done | bytes 491536 | tf_op jit(solution)/shard_map/reduce_scatter | solution.py:107
  384.4 4.3 %all-to-all-start.3 = ((bf16[4,12,5120]{2,1,0:T(8,128)(2,1)}), bf16[4,12,5120]{2,1,0:T(8,128)(2,1)S(1)}, u32[]{:S(2)}, u32[]{:S(2)}) async-start(bf16[4,12,5120]{2,1,0:T(8,128)(2,1)} %reshape.76), calls=%async_computation.4 | async-start | bytes 1310720 | tf_op jit(solution)/shard_map/all_to_all | solution.py:113
  388.7 9.6 %all-to-all-done.3 = bf16[4,12,5120]{2,1,0:T(8,128)(2,1)S(1)} async-done(((bf16[4,12,5120]{2,1,0:T(8,128)(2,1)}), bf16[4,12,5120]{2,1,0:T(8,128)(2,1)S(1)}, u32[]{:S(2)}, u32[]{:S(2)}) %all-to-all-start.3) | async-done | bytes 491552 | tf_op jit(solution)/shard_map/all_to_all | solution.py:113
  399.2 2.1 fusion.6
  (37 shorter events, 12.0 us)
Async XLA Ops:
  6.5 239.6 %copy-start = (bf16[1,256,5120]{2,1,0:T(8,128)(2,1)S(1)}, bf16[1,256,5120]{2,1,0:T(8,128)(2,1)}, u32[]{:S(2)}) copy-start(bf16[1,256,5120]{2,1,0:T(8,128)(2,1)} %param.19) | copy-start | bytes 7864324
  10.7 8.6 %copy-start.3 = (bf16[128,1280]{1,0:T(8,128)(2,1)S(1)}, bf16[128,1280]{1,0:T(8,128)(2,1)}, u32[]{:S(2)}) copy-start(bf16[128,1280]{1,0:T(8,128)(2,1)} %param.10) | copy-start | bytes 983044
  10.7 62.5 %all-to-all-start = ((bf16[32,2,128,256]{2,3,1,0:T(8,128)(2,1)}), bf16[32,2,128,256]{2,3,1,0:T(8,128)(2,1)}, u32[]{:S(2)}, u32[]{:S(2)}) async-start(bf16[32,2,128,256]{2,3,1,0:T(8,128)(2,1)} %stack.2), calls=%async_computation | async-start | bytes 8388608 | tf_op jit(solution)/shard_map/all_to_all | solution.py:46
  97.5 7.0 %copy-start.1 = (f32[2,4096,128,5]{2,1,3,0:T(8,128)}, f32[2,4096,128,5]{2,1,3,0:T(8,128)S(1)}, u32[]{:S(2)}) copy-start(f32[2,4096,128,5]{2,1,3,0:T(8,128)S(1)} %get-tuple-element.10) | copy-start | bytes 62914564
  117.6 12.4 %copy-start.5 = (s32[32,1]{0,1:T(1,128)S(1)}, s32[32,1]{0,1:T(1,128)}, u32[]{:S(2)}) copy-start(s32[32,1]{0,1:T(1,128)} %param.15) | copy-start | bytes 388
  125.3 21.3 %copy-start.4 = (bf16[32,5120]{1,0:T(8,128)(2,1)S(1)}, bf16[32,5120]{1,0:T(8,128)(2,1)}, u32[]{:S(2)}) copy-start(bf16[32,5120]{1,0:T(8,128)(2,1)} %param.12) | copy-start | bytes 983044
  125.3 21.6 %copy-start.6 = (f32[32]{0:T(128)S(1)}, f32[32]{0:T(128)}, u32[]{:S(2)}) copy-start(f32[32]{0:T(128)} %param.14) | copy-start | bytes 388
  125.3 22.3 %copy-start.7 = (f32[5120]{0:T(1024)S(1)}, f32[5120]{0:T(1024)}, u32[]{:S(2)}) copy-start(f32[5120]{0:T(1024)} %param.13) | copy-start | bytes 61444
  125.3 19.7 %all-to-all-start.1 = ((bf16[4,32,5120]{2,1,0:T(8,128)(2,1)}), bf16[4,32,5120]{2,1,0:T(8,128)(2,1)}, u32[]{:S(2)}, u32[]{:S(2)}) async-start(bf16[4,32,5120]{2,1,0:T(8,128)(2,1)} %bitcast.79), calls=%async_computation.1 | async-start | bytes 2621440 | tf_op jit(solution)/shard_map/all_to_all | solution.py:18
  129.9 104.5 %all-gather.2.cloned.1.call-start = ((), (), s32[]{:S(2)}) async-start(), calls=%async_computation.5 | async-start | bytes 16220160 | tf_op jit(solution)/shard_map/all_gather | solution.py:102
  146.9 0.7 copy-start.2
  163.8 218.7 %reduce-scatter.2.cloned.1.call-start = ((), (), s32[]{:S(2)}) async-start(), calls=%async_computation.6 | async-start | bytes 16220160 | tf_op jit(solution)/shard_map/reduce_scatter | solution.py:107
  384.4 13.9 %all-to-all-start.3 = ((bf16[4,12,5120]{2,1,0:T(8,128)(2,1)}), bf16[4,12,5120]{2,1,0:T(8,128)(2,1)S(1)}, u32[]{:S(2)}, u32[]{:S(2)}) async-start(bf16[4,12,5120]{2,1,0:T(8,128)(2,1)} %reshape.76), calls=%async_computation.4 | async-start | bytes 1310720 | tf_op jit(solution)/shard_map/all_to_all | solution.py:113
Sparse Core Ops, SparseCore 0:
  163.9 70.4 all-gather.1
  270.1 112.3 reduce-scatter.1
